TPU v7x, 32 devices: a whole 2x2x4 slice. The times are simulated.
32 devices in a mesh: px: 4 (over x, core), py: 8 (over z, y).
Axes of the slice: x: 2, y: 2, z: 4, core: 2. Of those that a mesh axis runs over, the one named last changes fastest.
Arguments:
- fraction: float32 [32, 64, 640], P('px', 'py'), may hold values from 0 to 1
- courant_x: float32 [32, 64, 640], P('px', 'py'), may hold values from -0.5 to 0.5
- courant_y: float32 [32, 64, 640], P('px', 'py'), may hold values from -0.5 to 0.5
- courant_z: float32 [32, 64, 640], P('px', 'py'), may hold values from -0.5 to 0.5
- labels: int32 [32, 64, 640], P('px', 'py'), may hold values from -1 to 31, as said below
- structure_owner: int32 [4, 32], P('px'), may hold values from 0 to 7, as said below
- parcel_owner: int32 [4, 32], P('px'), may hold values from 0 to 7, as said below
Outputs:
- remaining: float32 [32, 64, 640], P('px', 'py')
- moments: float32 [4, 13, 32], P('px', None, 'py')
- parcels: float32 [4, 13, 32], P('px', None, 'py')
Inputs may be any that keep to these rules, and one draw needn't show every extreme that they name: `labels`: a label names a structure of the cell's row. `structure_owner`: in each row every index of py owns exactly 4 structures. `parcel_owner`: in each row every index of py receives exactly 4 parcels.
All inputs are finite; a program needn't handle non-finite values.
Results may differ from a plain program's by a relative error of at most 0.0003.
Values sent between devices are 32-bit elements; how exact they have to be, the bound alone decides.
A program may use at most 64 MiB of HBM per device.

v0:
```python
import math
import jax
import jax.numpy as jnp
from jax import lax
from jax.sharding import PartitionSpec as P


def with_halo(x, sides, width, wrap):
    for axis, dim in sides:
        size, length = (lax.axis_size(axis), x.shape[dim])
        up = [(i, (i + 1) % size) for i in range(size if wrap else size - 1)]
        down = [(j, i) for i, j in up]
        last = lax.slice_in_dim(x, length - width, length, axis=dim)
        initial = lax.slice_in_dim(x, 0, width, axis=dim)
        before = lax.ppermute(last, axis, up)
        after = lax.ppermute(initial, axis, down)
        x = jnp.concatenate([before, x, after], axis=dim)
    return x


def advance(padded_frac, padded_cour, length, axis):

    def part(array, start, count):
        return lax.slice_in_dim(array, start, start + count, axis=axis)

    centre = part(padded_frac, 1, length + 2)
    spread = 0.5 * (part(padded_frac, 2, length + 2) - part(padded_frac, 0, length + 2))
    bound = 2.0 * jnp.minimum(centre, 1.0 - centre)
    slope = jnp.minimum(jnp.maximum(spread, -bound), bound)
    courant = part(padded_cour, 1, length + 1)
    upwind = part(centre, 0, length + 1) + 0.5 * (1.0 - courant) * part(slope, 0, length + 1)
    downwind = part(centre, 1, length + 1) - 0.5 * (1.0 + courant) * part(slope, 1, length + 1)
    flux = courant * jnp.where(courant > 0.0, upwind, downwind)
    middle = part(padded_frac, 2, length)
    high = part(courant, 1, length)
    low = part(courant, 0, length)
    updated = middle - (part(flux, 1, length) - part(flux, 0, length)) + middle * (high - low)
    return (updated, 0.5 * (high + low))


def parcel_rows(moment_rows):
    volume = moment_rows[0]
    safe = jnp.maximum(volume, 0.5)
    centre = moment_rows[1:4] / safe
    velocity = moment_rows[4:7] / safe
    square = moment_rows[7:10] / safe - centre * centre
    cross = jnp.stack(
        [
            moment_rows[10] / safe - centre[0] * centre[1],
            moment_rows[11] / safe - centre[0] * centre[2],
            moment_rows[12] / safe - centre[1] * centre[2],
        ]
    )
    return jnp.concatenate([volume[None], centre, velocity, square, cross], 0)


def slot_table(owner_row, per_owner):
    count = owner_row.shape[0]
    index = jnp.arange(count, dtype=jnp.int32)
    same = owner_row[:, None] == owner_row[None, :]
    earlier = index[None, :] < index[:, None]
    rank = jnp.sum((same & earlier).astype(jnp.int32), axis=1)
    position = owner_row * per_owner + rank
    return (position[:, None] == index[None, :]).astype(jnp.float32)


def product(left, right):
    return jnp.dot(left, right, precision=lax.Precision.HIGHEST, preferred_element_type=jnp.float32)


def local(fraction, courant_x, courant_y, courant_z, labels, structure_owner, parcel_owner):
    rows_x, rows_y, depth = fraction.shape
    padded = with_halo(jnp.stack([fraction, courant_x]), (("px", 1),), 2, True)
    first, velocity_x = advance(padded[0], padded[1], rows_x, 0)
    padded_y = with_halo(jnp.stack([first, courant_y]), (("py", 2),), 2, False)
    second, velocity_y = advance(padded_y[0], padded_y[1], rows_y, 1)
    pad_z = ((0, 0), (0, 0), (2, 2))
    third, velocity_z = advance(jnp.pad(second, pad_z), jnp.pad(courant_z, pad_z), depth, 2)
    remaining = jnp.where(labels >= 0, jnp.float32(0.0), third)
    width_py = lax.axis_size("py")
    row_index = lax.axis_index("py")
    total_x = rows_x * lax.axis_size("px")
    total_y = rows_y * width_py
    structures = structure_owner.shape[1]
    per_owner = structures // width_py
    scale = 4.0 / (rows_x * rows_y * rows_y)
    start_x = lax.axis_index("px") * rows_x
    start_y = row_index * rows_y
    coord_x = ((start_x + jnp.arange(rows_x, dtype=jnp.int32)).astype(jnp.float32) + 0.5)[
        :, None, None
    ] / total_x
    coord_y = ((start_y + jnp.arange(rows_y, dtype=jnp.int32)).astype(jnp.float32) + 0.5)[
        None, :, None
    ] / total_y
    coord_z = (jnp.arange(depth, dtype=jnp.int32).astype(jnp.float32) + 0.5)[None, None, :] / depth
    weight = third * scale
    shape = weight.shape
    cells = rows_x * rows_y * depth
    block = math.gcd(cells, 4096)
    blocks = cells // block
    pieces = [
        jnp.ones(shape, jnp.float32),
        coord_x,
        coord_y,
        coord_z,
        velocity_x,
        velocity_y,
        velocity_z,
        coord_x * coord_x,
        coord_y * coord_y,
        coord_z * coord_z,
        coord_x * coord_y,
        coord_x * coord_z,
        coord_y * coord_z,
    ]
    feature_blocks = jnp.stack(
        [(weight * jnp.broadcast_to(piece, shape)).reshape(blocks, block) for piece in pieces], 1
    )
    label_blocks = labels.reshape(blocks, block)
    columns = jnp.arange(structures, dtype=jnp.int32)

    def accumulate(total, inputs):
        feature_rows, marks = inputs
        onehot = (marks[:, None] == columns[None, :]).astype(jnp.float32)
        return (total + product(feature_rows, onehot), None)

    partial_sums, unused = lax.scan(
        accumulate, jnp.zeros((13, structures), jnp.float32), (feature_blocks, label_blocks)
    )
    owner_slots = slot_table(structure_owner[0], per_owner)
    parcel_slots = slot_table(parcel_owner[0], per_owner)
    mine_owned = lax.dynamic_slice_in_dim(owner_slots, row_index * per_owner, per_owner, 1)
    totals = lax.psum(partial_sums, "py")
    owned = product(totals, mine_owned)
    mine_parcels = lax.dynamic_slice_in_dim(parcel_slots, row_index * per_owner, per_owner, 1)
    received = product(parcel_rows(totals), mine_parcels)
    return (remaining, owned[None], received[None])


def solution(mesh):
    return jax.shard_map(
        local,
        mesh=mesh,
        in_specs=(
            P("px", "py", None),
            P("px", "py", None),
            P("px", "py", None),
            P("px", "py", None),
            P("px", "py", None),
            P("px", None),
            P("px", None),
        ),
        out_specs=(P("px", "py", None), P("px", None, "py"), P("px", None, "py")),
        check_vma=False,
    )
```

profile of v0, /device:TPU:0, one launch (start us, length us, event | category | flops | bytes accessed | tf_op | source)
XLA Modules:
  0.0 86.4 jit_solution(18232538209815463961)
XLA Ops:
  1.6 2.5 %collective-permute-start.1 = (f32[2,2,8,640]{3,2,1,0:T(8,128)S(1)}, f32[2,2,8,640]{3,2,1,0:T(8,128)S(1)}, u32[]{:S(2)}, u32[]{:S(2)}) collective-permute-start(f32[2,2,8,640]{3,2,1,0:T(8,128)S(1)} %get-tuple-element.72), channel_id=1, source_target_pairs={{8,0},{16,8},{24,16},{0,24},{9,1},{17,9},{25,17},{1,25},{10,2},{18... | collective-permute-start | bytes 245768 | tf_op jit(solution)/shard_map/ppermute | solution.py:16
  4.2 1.7 %reshape.154 = s32[10,4096]{1,0:T(8,128)} reshape(s32[8,8,640]{2,1,0:T(8,128)} %param.13) | data formatting | bytes 327680 | tf_op jit(solution)/shard_map/reshape | solution.py:119
  9.0 1.2 %pad_maximum_fusion.1 = (f32[2,10,8,640]{3,2,1,0:T(8,128)S(1)}, f32[2,10,8,640]{3,2,1,0:T(8,128)S(1)}) fusion(f32[2,2,8,640]{3,2,1,0:T(8,128)S(1)} %collective-permute-done.1, f32[1,8,8,640]{3,2,1,0:T(8,128)} %bitcast.60, f32[1,8,8,640]{3,2,1,0:T(8,128)} %bitcast.64, f32[2,2,8,640]{3,2,1,0:T(8,128)S(1)} %collective-permute-done), kind=kLoop, calls=%fused_computation.12 | loop fusion | flops 409600 | bytes 1310720 | tf_op jit(solution)/shard_map/concatenate | solution.py:17
  10.3 1.0 %fusion.16 = f32[10,8,640]{2,1,0:T(8,128)S(1)} fusion(f32[2,10,8,640]{3,2,1,0:T(8,128)S(1)} %get-tuple-element.71, f32[2,10,8,640]{3,2,1,0:T(8,128)S(1)} %get-tuple-element.70, f32[2,2,8,640]{3,2,1,0:T(8,128)S(1)} %collective-permute-done.1, f32[1,8,8,640]{3,2,1,0:T(8,128)} %bitcast.61, f32[1,8,8,640]{3,2,1,0:T(8,128)} %bitcast.65, ...), kind=kLoop, calls=%fused_computation.42 | loop fusion | flops 563200 | bytes 1105920 | tf_op jit(solution)/shard_map/min | solution.py:29
  11.5 3.4 %collective-permute-start.2 = (f32[2,8,2,640]{3,2,1,0:T(2,128)S(1)}, f32[2,8,2,640]{3,2,1,0:T(2,128)S(1)}, u32[]{:S(2)}, u32[]{:S(2)}) collective-permute-start(f32[2,8,2,640]{3,2,1,0:T(2,128)S(1)} %get-tuple-element.68), channel_id=1, source_target_pairs={{0,1},{1,2},{2,3},{3,4},{4,5},{5,6},{6,7},{8,9},{9,10},{10,11},{11... | collective-permute-start | bytes 245768 | tf_op jit(solution)/shard_map/ppermute | solution.py:15
  14.9 1.3 %collective-permute-start.3 = (f32[2,8,2,640]{3,2,1,0:T(2,128)S(1)}, f32[2,8,2,640]{3,2,1,0:T(2,128)S(1)}, u32[]{:S(2)}, u32[]{:S(2)}) collective-permute-start(f32[2,8,2,640]{3,2,1,0:T(2,128)S(1)} %get-tuple-element.69), channel_id=1, source_target_pairs={{1,0},{2,1},{3,2},{4,3},{5,4},{6,5},{7,6},{9,8},{10,9},{11,10},{12... | collective-permute-start | bytes 245768 | tf_op jit(solution)/shard_map/ppermute | solution.py:16
  16.2 1.3 %collective-permute-done.2 = f32[2,8,2,640]{3,2,1,0:T(2,128)S(1)} collective-permute-done((f32[2,8,2,640]{3,2,1,0:T(2,128)S(1)}, f32[2,8,2,640]{3,2,1,0:T(2,128)S(1)}, u32[]{:S(2)}, u32[]{:S(2)}) %collective-permute-start.2) | collective-permute-done | bytes 81952 | tf_op jit(solution)/shard_map/ppermute | solution.py:15
  17.5 4.1 %collective-permute-done.3 = f32[2,8,2,640]{3,2,1,0:T(2,128)S(1)} collective-permute-done((f32[2,8,2,640]{3,2,1,0:T(2,128)S(1)}, f32[2,8,2,640]{3,2,1,0:T(2,128)S(1)}, u32[]{:S(2)}, u32[]{:S(2)}) %collective-permute-start.3) | collective-permute-done | bytes 81952 | tf_op jit(solution)/shard_map/ppermute | solution.py:16
  33.7 30.6 %while.11 = (s32[]{:T(128)}, f32[13,32]{1,0:T(8,128)S(1)}, f32[10,13,4096]{2,0,1:T(8,128)}, s32[10,4096]{1,0:T(8,128)}, s32[]{:T(128)}, /*index=5*/s32[]{:T(128)}) while((s32[]{:T(128)}, f32[13,32]{1,0:T(8,128)S(1)}, f32[10,13,4096]{2,0,1:T(8,128)}, s32[10,4096]{1,0:T(8,128)}, s32[]{:T(128)}, /*index=5*/s32[]{:T(128)}) %tuple.55), condition=%wide.region_1.2_spmd.clone, body=%wide.region_0.1_spmd.clone.sunk | while | flops 20579140 | bytes 691543 | solution.py:127
  33.7 1.6 %constant_dynamic-slice_fusion.4 = f32[1,13,4096]{2,0,1:T(1,128)S(1)} fusion(f32[10,13,4096]{2,0,1:T(8,128)} %get-tuple-element.143, s32[]{:T(128)} %get-tuple-element.135), kind=kLoop, calls=%fused_computation.6.clone.1 | loop fusion | bytes 425988 | tf_op jit(solution)/shard_map/while/body/jit(dynamic_index_in_dim)/dynamic_slice | solution.py:127
  35.4 0.9 %constant_dynamic-slice_fusion.5 = s32[1,4096]{1,0:T(1,128)S(1)} fusion(s32[10,4096]{1,0:T(8,128)} %get-tuple-element.144, s32[]{:T(128)} %get-tuple-element.135), kind=kLoop, calls=%fused_computation.5.clone.1 | loop fusion | bytes 32772 | tf_op jit(solution)/shard_map/while/body/jit(dynamic_index_in_dim)/dynamic_slice | solution.py:127
  36.8 1.6 %constant_dynamic-slice_fusion.4 = f32[1,13,4096]{2,0,1:T(1,128)S(1)} fusion(f32[10,13,4096]{2,0,1:T(8,128)} %get-tuple-element.143, s32[]{:T(128)} %get-tuple-element.135), kind=kLoop, calls=%fused_computation.6.clone.1 | loop fusion | bytes 425988 | tf_op jit(solution)/shard_map/while/body/jit(dynamic_index_in_dim)/dynamic_slice | solution.py:127
  38.5 0.9 %constant_dynamic-slice_fusion.5 = s32[1,4096]{1,0:T(1,128)S(1)} fusion(s32[10,4096]{1,0:T(8,128)} %get-tuple-element.144, s32[]{:T(128)} %get-tuple-element.135), kind=kLoop, calls=%fused_computation.5.clone.1 | loop fusion | bytes 32772 | tf_op jit(solution)/shard_map/while/body/jit(dynamic_index_in_dim)/dynamic_slice | solution.py:127
  39.9 1.6 %constant_dynamic-slice_fusion.4 = f32[1,13,4096]{2,0,1:T(1,128)S(1)} fusion(f32[10,13,4096]{2,0,1:T(8,128)} %get-tuple-element.143, s32[]{:T(128)} %get-tuple-element.135), kind=kLoop, calls=%fused_computation.6.clone.1 | loop fusion | bytes 425988 | tf_op jit(solution)/shard_map/while/body/jit(dynamic_index_in_dim)/dynamic_slice | solution.py:127
  41.5 0.9 %constant_dynamic-slice_fusion.5 = s32[1,4096]{1,0:T(1,128)S(1)} fusion(s32[10,4096]{1,0:T(8,128)} %get-tuple-element.144, s32[]{:T(128)} %get-tuple-element.135), kind=kLoop, calls=%fused_computation.5.clone.1 | loop fusion | bytes 32772 | tf_op jit(solution)/shard_map/while/body/jit(dynamic_index_in_dim)/dynamic_slice | solution.py:127
  42.9 1.6 %constant_dynamic-slice_fusion.4 = f32[1,13,4096]{2,0,1:T(1,128)S(1)} fusion(f32[10,13,4096]{2,0,1:T(8,128)} %get-tuple-element.143, s32[]{:T(128)} %get-tuple-element.135), kind=kLoop, calls=%fused_computation.6.clone.1 | loop fusion | bytes 425988 | tf_op jit(solution)/shard_map/while/body/jit(dynamic_index_in_dim)/dynamic_slice | solution.py:127
  44.6 0.9 %constant_dynamic-slice_fusion.5 = s32[1,4096]{1,0:T(1,128)S(1)} fusion(s32[10,4096]{1,0:T(8,128)} %get-tuple-element.144, s32[]{:T(128)} %get-tuple-element.135), kind=kLoop, calls=%fused_computation.5.clone.1 | loop fusion | bytes 32772 | tf_op jit(solution)/shard_map/while/body/jit(dynamic_index_in_dim)/dynamic_slice | solution.py:127
  46.0 1.6 %constant_dynamic-slice_fusion.4 = f32[1,13,4096]{2,0,1:T(1,128)S(1)} fusion(f32[10,13,4096]{2,0,1:T(8,128)} %get-tuple-element.143, s32[]{:T(128)} %get-tuple-element.135), kind=kLoop, calls=%fused_computation.6.clone.1 | loop fusion | bytes 425988 | tf_op jit(solution)/shard_map/while/body/jit(dynamic_index_in_dim)/dynamic_slice | solution.py:127
  49.1 1.6 %constant_dynamic-slice_fusion.4 = f32[1,13,4096]{2,0,1:T(1,128)S(1)} fusion(f32[10,13,4096]{2,0,1:T(8,128)} %get-tuple-element.143, s32[]{:T(128)} %get-tuple-element.135), kind=kLoop, calls=%fused_computation.6.clone.1 | loop fusion | bytes 425988 | tf_op jit(solution)/shard_map/while/body/jit(dynamic_index_in_dim)/dynamic_slice | solution.py:127
  52.1 1.6 %constant_dynamic-slice_fusion.4 = f32[1,13,4096]{2,0,1:T(1,128)S(1)} fusion(f32[10,13,4096]{2,0,1:T(8,128)} %get-tuple-element.143, s32[]{:T(128)} %get-tuple-element.135), kind=kLoop, calls=%fused_computation.6.clone.1 | loop fusion | bytes 425988 | tf_op jit(solution)/shard_map/while/body/jit(dynamic_index_in_dim)/dynamic_slice | solution.py:127
  55.2 1.6 %constant_dynamic-slice_fusion.4 = f32[1,13,4096]{2,0,1:T(1,128)S(1)} fusion(f32[10,13,4096]{2,0,1:T(8,128)} %get-tuple-element.143, s32[]{:T(128)} %get-tuple-element.135), kind=kLoop, calls=%fused_computation.6.clone.1 | loop fusion | bytes 425988 | tf_op jit(solution)/shard_map/while/body/jit(dynamic_index_in_dim)/dynamic_slice | solution.py:127
  58.3 1.6 %constant_dynamic-slice_fusion.4 = f32[1,13,4096]{2,0,1:T(1,128)S(1)} fusion(f32[10,13,4096]{2,0,1:T(8,128)} %get-tuple-element.143, s32[]{:T(128)} %get-tuple-element.135), kind=kLoop, calls=%fused_computation.6.clone.1 | loop fusion | bytes 425988 | tf_op jit(solution)/shard_map/while/body/jit(dynamic_index_in_dim)/dynamic_slice | solution.py:127
  61.3 1.6 %constant_dynamic-slice_fusion.4 = f32[1,13,4096]{2,0,1:T(1,128)S(1)} fusion(f32[10,13,4096]{2,0,1:T(8,128)} %get-tuple-element.143, s32[]{:T(128)} %get-tuple-element.135), kind=kLoop, calls=%fused_computation.6.clone.1 | loop fusion | bytes 425988 | tf_op jit(solution)/shard_map/while/body/jit(dynamic_index_in_dim)/dynamic_slice | solution.py:127
  64.4 20.1 %psum.7 = f32[13,32]{1,0:T(8,128)S(1)} all-reduce(f32[13,32]{1,0:T(8,128)S(1)} %get-tuple-element.30), channel_id=1, replica_groups=mesh['px'=4,'py'=8] {'py'}, use_global_device_ids=true, to_apply=%region_2.3 | all-reduce | flops 416 | bytes 3328 | tf_op jit(solution)/shard_map/psum | solution.py:133
  (86 shorter events, 28.4 us)
Async XLA Ops:
  0.6 10.6 %copy-start.1 = (f32[8,8,640]{2,1,0:T(8,128)S(1)}, f32[8,8,640]{2,1,0:T(8,128)}, u32[]{:S(2)}) copy-start(f32[8,8,640]{2,1,0:T(8,128)} %param.9) | copy-start | bytes 491524
  0.6 10.6 %copy-start = (f32[8,8,640]{2,1,0:T(8,128)S(1)}, f32[8,8,640]{2,1,0:T(8,128)}, u32[]{:S(2)}) copy-start(f32[8,8,640]{2,1,0:T(8,128)} %param.10) | copy-start | bytes 491524
  0.7 10.8 %copy-start.4 = (f32[8,8,640]{2,1,0:T(8,128)S(1)}, f32[8,8,640]{2,1,0:T(8,128)}, u32[]{:S(2)}) copy-start(f32[8,8,640]{2,1,0:T(8,128)} %param.11) | copy-start | bytes 491524
  1.6 7.5 %collective-permute-start.1 = (f32[2,2,8,640]{3,2,1,0:T(8,128)S(1)}, f32[2,2,8,640]{3,2,1,0:T(8,128)S(1)}, u32[]{:S(2)}, u32[]{:S(2)}) collective-permute-start(f32[2,2,8,640]{3,2,1,0:T(8,128)S(1)} %get-tuple-element.72), channel_id=1, source_target_pairs={{8,0},{16,8},{24,16},{0,24},{9,1},{17,9},{25,17},{1,25},{10,2},{18... | collective-permute-start | bytes 245768 | tf_op jit(solution)/shard_map/ppermute | solution.py:16
  4.0 5.0 %collective-permute-start = (f32[2,2,8,640]{3,2,1,0:T(8,128)S(1)}, f32[2,2,8,640]{3,2,1,0:T(8,128)S(1)}, u32[]{:S(2)}, u32[]{:S(2)}) collective-permute-start(f32[2,2,8,640]{3,2,1,0:T(8,128)S(1)} %get-tuple-element.73), channel_id=1, source_target_pairs={{0,8},{8,16},{16,24},{24,0},{1,9},{9,17},{17,25},{25,1},{2,10},{10... | collective-permute-start | bytes 245768 | tf_op jit(solution)/shard_map/ppermute | solution.py:15
  11.5 6.0 %collective-permute-start.2 = (f32[2,8,2,640]{3,2,1,0:T(2,128)S(1)}, f32[2,8,2,640]{3,2,1,0:T(2,128)S(1)}, u32[]{:S(2)}, u32[]{:S(2)}) collective-permute-start(f32[2,8,2,640]{3,2,1,0:T(2,128)S(1)} %get-tuple-element.68), channel_id=1, source_target_pairs={{0,1},{1,2},{2,3},{3,4},{4,5},{5,6},{6,7},{8,9},{9,10},{10,11},{11... | collective-permute-start | bytes 245768 | tf_op jit(solution)/shard_map/ppermute | solution.py:15
  14.9 6.7 %collective-permute-start.3 = (f32[2,8,2,640]{3,2,1,0:T(2,128)S(1)}, f32[2,8,2,640]{3,2,1,0:T(2,128)S(1)}, u32[]{:S(2)}, u32[]{:S(2)}) collective-permute-start(f32[2,8,2,640]{3,2,1,0:T(2,128)S(1)} %get-tuple-element.69), channel_id=1, source_target_pairs={{1,0},{2,1},{3,2},{4,3},{5,4},{6,5},{7,6},{9,8},{10,9},{11,10},{12... | collective-permute-start | bytes 245768 | tf_op jit(solution)/shard_map/ppermute | solution.py:16
  16.2 6.2 %copy-start.2 = (f32[8,8,640]{2,1,0:T(8,128)S(1)}, f32[8,8,640]{2,1,0:T(8,128)}, u32[]{:S(2)}) copy-start(f32[8,8,640]{2,1,0:T(8,128)} %param.12) | copy-start | bytes 491524
  21.8 1.0 %copy-start.3 = (s32[8,8,640]{2,1,0:T(8,128)S(1)}, s32[8,8,640]{2,1,0:T(8,128)}, u32[]{:S(2)}) copy-start(s32[8,8,640]{2,1,0:T(8,128)} %param.13) | copy-start | bytes 491524
where the time goes:
time: 87.1 us; the launch traced here: 86.4 us
  local copies, waits for them, and re-layouts  37.5 us (43%)
  blocking collectives  20.1 us (23%)
  other arithmetic  8.61 us (10%)
  starting transfers between devices  7.18 us (8%)
  matrix products  6.3 us (7%)
  waiting for transfers between devices  5.37 us (6%)
  between operations  0.97 us (1%)
    dynamic_slice x20, local copies, waits for them, and re-layouts, local(): lax.scan(accumulate, jnp.zeros((13, structures), jnp.float32), (feature_b...  25.7 us
    psum x1, blocking collectives, local(): totals = lax.psum(partial_sums, 'py')  20.1 us
    unnamed x22, local copies, waits for them, and re-layouts  8.8 us
    dot_general x12, matrix products, product(): jnp.dot(left, right, precision=lax.Precision.HIGHEST, preferred_element_t...  6.3 us
    ppermute x2, waiting for transfers between devices, with_halo(): after = lax.ppermute(initial, axis, down)  4.12 us
    ppermute x2, starting transfers between devices, with_halo(): after = lax.ppermute(initial, axis, down)  3.75 us
    ppermute x2, starting transfers between devices, with_halo(): before = lax.ppermute(last, axis, up)  3.43 us
    reduce_sum x2, other arithmetic, slot_table(): rank = jnp.sum((same & earlier).astype(jnp.int32), axis=1)  1.82 us
  transfers between devices with their start and end apart: 4, of which 2 were waited for; matrix products, arithmetic and copies ran while one was open for 6% of the time, Pallas kernels for 0%

commit v1 on v0

--- a/solution.py
+++ b/solution.py
@@ -3,6 +3,15 @@
 import jax.numpy as jnp
 from jax import lax
 from jax.sharding import PartitionSpec as P
+
+
+def doubling_sum(block, name):
+    size = lax.axis_size(name)
+    total, reach = (block, 1)
+    while reach < size:
+        total = total + lax.ppermute(total, name, [(i, i ^ reach) for i in range(size)])
+        reach = 2 * reach
+    return total
 
 
 def with_halo(x, sides, width, wrap):
@@ -130,7 +139,7 @@
     owner_slots = slot_table(structure_owner[0], per_owner)
     parcel_slots = slot_table(parcel_owner[0], per_owner)
     mine_owned = lax.dynamic_slice_in_dim(owner_slots, row_index * per_owner, per_owner, 1)
-    totals = lax.psum(partial_sums, "py")
+    totals = doubling_sum(partial_sums, "py")
     owned = product(totals, mine_owned)
     mine_parcels = lax.dynamic_slice_in_dim(parcel_slots, row_index * per_owner, per_owner, 1)
     received = product(parcel_rows(totals), mine_parcels)

time: 87.1 us -> 77.6 us (0.89)
  blocking collectives: 20.1 us -> 0 us
  starting transfers between devices: 7.18 us -> 13.8 us
  waiting for transfers between devices: 5.37 us -> 11.6 us
  other arithmetic: 8.61 us -> 6.56 us
    psum x1 -> x0, blocking collectives: 20.1 us -> none  [local(): totals = lax.psum(partial_sums, 'py')]
    ppermute x0 -> x3, starting transfers between devices: none -> 6.64 us  [doubling_sum(): lax.ppermute(total, name, [(i, i ^ reach) for i in range(size)])]
    ppermute x0 -> x3, waiting for transfers between devices: none -> 5.49 us  [doubling_sum(): lax.ppermute(total, name, [(i, i ^ reach) for i in range(size)])]
    add x2, other arithmetic: 1.33 us -> 0.01 us  [slot_table(): position = owner_row * per_owner + rank]
    unnamed x22 -> x26, local copies, waits for them, and re-layouts: 8.8 us -> 8.67 us
  transfers between devices with their start and end apart: 4 -> 7, of which waited for: 2 -> 6; matrix products, arithmetic and copies ran while one was open for 6% -> 4% of each run, Pallas kernels for 0% -> 0%
where the time goes in v1:
time: 77.6 us; the launch traced here: 76.9 us
  local copies, waits for them, and re-layouts  37.3 us (48%)
  starting transfers between devices  13.8 us (18%)
  waiting for transfers between devices  11.6 us (15%)
  other arithmetic  6.56 us (8%)
  matrix products  6.3 us (8%)
  between operations  0.95 us (1%)
    dynamic_slice x20, local copies, waits for them, and re-layouts, local(): lax.scan(accumulate, jnp.zeros((13, structures), jnp.float32), (feature_b...  25.7 us
    unnamed x26, local copies, waits for them, and re-layouts  8.67 us
    ppermute x3, starting transfers between devices, doubling_sum(): lax.ppermute(total, name, [(i, i ^ reach) for i in range(size)])  6.64 us
    dot_general x12, matrix products, product(): jnp.dot(left, right, precision=lax.Precision.HIGHEST, preferred_element_t...  6.3 us
    ppermute x3, waiting for transfers between devices, doubling_sum(): lax.ppermute(total, name, [(i, i ^ reach) for i in range(size)])  5.49 us
    ppermute x2, waiting for transfers between devices, with_halo(): after = lax.ppermute(initial, axis, down)  4.31 us
    ppermute x2, starting transfers between devices, with_halo(): after = lax.ppermute(initial, axis, down)  3.75 us
    ppermute x2, starting transfers between devices, with_halo(): before = lax.ppermute(last, axis, up)  3.43 us
  transfers between devices with their start and end apart: 7, of which 6 were waited for; matrix products, arithmetic and copies ran while one was open for 4% of the time, Pallas kernels for 0%

profile of v1, /device:TPU:0, one launch (start us, length us, event | category | flops | bytes accessed | tf_op | source)
XLA Modules:
  0.0 76.9 jit_solution(15022045857597489059)
XLA Ops:
  1.6 2.5 %collective-permute-start.1 = (f32[2,2,8,640]{3,2,1,0:T(8,128)S(1)}, f32[2,2,8,640]{3,2,1,0:T(8,128)S(1)}, u32[]{:S(2)}, u32[]{:S(2)}) collective-permute-start(f32[2,2,8,640]{3,2,1,0:T(8,128)S(1)} %get-tuple-element.72), channel_id=1, source_target_pairs={{8,0},{16,8},{24,16},{0,24},{9,1},{17,9},{25,17},{1,25},{10,2},{18... | collective-permute-start | bytes 245768 | tf_op jit(solution)/shard_map/ppermute | solution.py:25
  4.2 1.7 %reshape.154 = s32[10,4096]{1,0:T(8,128)} reshape(s32[8,8,640]{2,1,0:T(8,128)} %param.13) | data formatting | bytes 327680 | tf_op jit(solution)/shard_map/reshape | solution.py:128
  6.8 1.1 %collective-permute-done = f32[2,2,8,640]{3,2,1,0:T(8,128)S(1)} collective-permute-done((f32[2,2,8,640]{3,2,1,0:T(8,128)S(1)}, f32[2,2,8,640]{3,2,1,0:T(8,128)S(1)}, u32[]{:S(2)}, u32[]{:S(2)}) %collective-permute-start) | collective-permute-done | bytes 81952 | tf_op jit(solution)/shard_map/ppermute | solution.py:24
  7.9 1.2 %pad_maximum_fusion.1 = (f32[2,10,8,640]{3,2,1,0:T(8,128)S(1)}, f32[2,10,8,640]{3,2,1,0:T(8,128)S(1)}) fusion(f32[2,2,8,640]{3,2,1,0:T(8,128)S(1)} %collective-permute-done.1, f32[1,8,8,640]{3,2,1,0:T(8,128)} %bitcast.60, f32[1,8,8,640]{3,2,1,0:T(8,128)} %bitcast.64, f32[2,2,8,640]{3,2,1,0:T(8,128)S(1)} %collective-permute-done), kind=kLoop, calls=%fused_computation.12 | loop fusion | flops 409600 | bytes 1310720 | tf_op jit(solution)/shard_map/concatenate | solution.py:26
  10.3 3.4 %collective-permute-start.2 = (f32[2,8,2,640]{3,2,1,0:T(2,128)S(1)}, f32[2,8,2,640]{3,2,1,0:T(2,128)S(1)}, u32[]{:S(2)}, u32[]{:S(2)}) collective-permute-start(f32[2,8,2,640]{3,2,1,0:T(2,128)S(1)} %get-tuple-element.68), channel_id=1, source_target_pairs={{0,1},{1,2},{2,3},{3,4},{4,5},{5,6},{6,7},{8,9},{9,10},{10,11},{11... | collective-permute-start | bytes 245768 | tf_op jit(solution)/shard_map/ppermute | solution.py:24
  13.8 1.3 %collective-permute-start.3 = (f32[2,8,2,640]{3,2,1,0:T(2,128)S(1)}, f32[2,8,2,640]{3,2,1,0:T(2,128)S(1)}, u32[]{:S(2)}, u32[]{:S(2)}) collective-permute-start(f32[2,8,2,640]{3,2,1,0:T(2,128)S(1)} %get-tuple-element.69), channel_id=1, source_target_pairs={{1,0},{2,1},{3,2},{4,3},{5,4},{6,5},{7,6},{9,8},{10,9},{11,10},{12... | collective-permute-start | bytes 245768 | tf_op jit(solution)/shard_map/ppermute | solution.py:25
  15.8 4.3 %collective-permute-done.3 = f32[2,8,2,640]{3,2,1,0:T(2,128)S(1)} collective-permute-done((f32[2,8,2,640]{3,2,1,0:T(2,128)S(1)}, f32[2,8,2,640]{3,2,1,0:T(2,128)S(1)}, u32[]{:S(2)}, u32[]{:S(2)}) %collective-permute-start.3) | collective-permute-done | bytes 81952 | tf_op jit(solution)/shard_map/ppermute | solution.py:25
  32.1 30.6 %while.11 = (s32[]{:T(128)}, f32[13,32]{1,0:T(8,128)S(1)}, f32[10,13,4096]{2,0,1:T(8,128)}, s32[10,4096]{1,0:T(8,128)}, s32[]{:T(128)}, /*index=5*/s32[]{:T(128)}) while((s32[]{:T(128)}, f32[13,32]{1,0:T(8,128)S(1)}, f32[10,13,4096]{2,0,1:T(8,128)}, s32[10,4096]{1,0:T(8,128)}, s32[]{:T(128)}, /*index=5*/s32[]{:T(128)}) %tuple.55), condition=%wide.region_1.2_spmd.clone, body=%wide.region_0.1_spmd.clone.sunk | while | flops 20579140 | bytes 691543 | solution.py:136
  32.1 1.6 %constant_dynamic-slice_fusion.4 = f32[1,13,4096]{2,0,1:T(1,128)S(1)} fusion(f32[10,13,4096]{2,0,1:T(8,128)} %get-tuple-element.143, s32[]{:T(128)} %get-tuple-element.135), kind=kLoop, calls=%fused_computation.6.clone.1 | loop fusion | bytes 425988 | tf_op jit(solution)/shard_map/while/body/jit(dynamic_index_in_dim)/dynamic_slice | solution.py:136
  35.1 1.6 %constant_dynamic-slice_fusion.4 = f32[1,13,4096]{2,0,1:T(1,128)S(1)} fusion(f32[10,13,4096]{2,0,1:T(8,128)} %get-tuple-element.143, s32[]{:T(128)} %get-tuple-element.135), kind=kLoop, calls=%fused_computation.6.clone.1 | loop fusion | bytes 425988 | tf_op jit(solution)/shard_map/while/body/jit(dynamic_index_in_dim)/dynamic_slice | solution.py:136
  38.2 1.6 %constant_dynamic-slice_fusion.4 = f32[1,13,4096]{2,0,1:T(1,128)S(1)} fusion(f32[10,13,4096]{2,0,1:T(8,128)} %get-tuple-element.143, s32[]{:T(128)} %get-tuple-element.135), kind=kLoop, calls=%fused_computation.6.clone.1 | loop fusion | bytes 425988 | tf_op jit(solution)/shard_map/while/body/jit(dynamic_index_in_dim)/dynamic_slice | solution.py:136
  41.3 1.6 %constant_dynamic-slice_fusion.4 = f32[1,13,4096]{2,0,1:T(1,128)S(1)} fusion(f32[10,13,4096]{2,0,1:T(8,128)} %get-tuple-element.143, s32[]{:T(128)} %get-tuple-element.135), kind=kLoop, calls=%fused_computation.6.clone.1 | loop fusion | bytes 425988 | tf_op jit(solution)/shard_map/while/body/jit(dynamic_index_in_dim)/dynamic_slice | solution.py:136
  44.4 1.6 %constant_dynamic-slice_fusion.4 = f32[1,13,4096]{2,0,1:T(1,128)S(1)} fusion(f32[10,13,4096]{2,0,1:T(8,128)} %get-tuple-element.143, s32[]{:T(128)} %get-tuple-element.135), kind=kLoop, calls=%fused_computation.6.clone.1 | loop fusion | bytes 425988 | tf_op jit(solution)/shard_map/while/body/jit(dynamic_index_in_dim)/dynamic_slice | solution.py:136
  47.4 1.6 %constant_dynamic-slice_fusion.4 = f32[1,13,4096]{2,0,1:T(1,128)S(1)} fusion(f32[10,13,4096]{2,0,1:T(8,128)} %get-tuple-element.143, s32[]{:T(128)} %get-tuple-element.135), kind=kLoop, calls=%fused_computation.6.clone.1 | loop fusion | bytes 425988 | tf_op jit(solution)/shard_map/while/body/jit(dynamic_index_in_dim)/dynamic_slice | solution.py:136
  50.5 1.6 %constant_dynamic-slice_fusion.4 = f32[1,13,4096]{2,0,1:T(1,128)S(1)} fusion(f32[10,13,4096]{2,0,1:T(8,128)} %get-tuple-element.143, s32[]{:T(128)} %get-tuple-element.135), kind=kLoop, calls=%fused_computation.6.clone.1 | loop fusion | bytes 425988 | tf_op jit(solution)/shard_map/while/body/jit(dynamic_index_in_dim)/dynamic_slice | solution.py:136
  53.6 1.6 %constant_dynamic-slice_fusion.4 = f32[1,13,4096]{2,0,1:T(1,128)S(1)} fusion(f32[10,13,4096]{2,0,1:T(8,128)} %get-tuple-element.143, s32[]{:T(128)} %get-tuple-element.135), kind=kLoop, calls=%fused_computation.6.clone.1 | loop fusion | bytes 425988 | tf_op jit(solution)/shard_map/while/body/jit(dynamic_index_in_dim)/dynamic_slice | solution.py:136
  56.6 1.6 %constant_dynamic-slice_fusion.4 = f32[1,13,4096]{2,0,1:T(1,128)S(1)} fusion(f32[10,13,4096]{2,0,1:T(8,128)} %get-tuple-element.143, s32[]{:T(128)} %get-tuple-element.135), kind=kLoop, calls=%fused_computation.6.clone.1 | loop fusion | bytes 425988 | tf_op jit(solution)/shard_map/while/body/jit(dynamic_index_in_dim)/dynamic_slice | solution.py:136
  59.7 1.6 %constant_dynamic-slice_fusion.4 = f32[1,13,4096]{2,0,1:T(1,128)S(1)} fusion(f32[10,13,4096]{2,0,1:T(8,128)} %get-tuple-element.143, s32[]{:T(128)} %get-tuple-element.135), kind=kLoop, calls=%fused_computation.6.clone.1 | loop fusion | bytes 425988 | tf_op jit(solution)/shard_map/while/body/jit(dynamic_index_in_dim)/dynamic_slice | solution.py:136
  62.7 2.5 %collective-permute-start.4 = (f32[13,32]{1,0:T(8,128)S(1)}, f32[13,32]{1,0:T(8,128)S(1)}, u32[]{:S(2)}, u32[]{:S(2)}) collective-permute-start(f32[13,32]{1,0:T(8,128)S(1)} %get-tuple-element.30), channel_id=1, source_target_pairs={{0,1},{1,0},{2,3},{3,2},{4,5},{5,4},{6,7},{7,6},{8,9},{9,8},{10,11... | collective-permute-start | bytes 5000 | tf_op jit(solution)/shard_map/ppermute | solution.py:12
  65.2 1.6 %collective-permute-done.4 = f32[13,32]{1,0:T(8,128)S(1)} collective-permute-done((f32[13,32]{1,0:T(8,128)S(1)}, f32[13,32]{1,0:T(8,128)S(1)}, u32[]{:S(2)}, u32[]{:S(2)}) %collective-permute-start.4) | collective-permute-done | bytes 1696 | tf_op jit(solution)/shard_map/ppermute | solution.py:12
  66.9 1.6 %collective-permute-start.5 = (f32[13,32]{1,0:T(8,128)S(1)}, f32[13,32]{1,0:T(8,128)S(1)}, u32[]{:S(2)}, u32[]{:S(2)}) collective-permute-start(f32[13,32]{1,0:T(8,128)S(1)} %add.170), channel_id=1, source_target_pairs={{0,2},{1,3},{2,0},{3,1},{4,6},{5,7},{6,4},{7,5},{8,10},{9,11},{10,... | collective-permute-start | bytes 5000 | tf_op jit(solution)/shard_map/ppermute | solution.py:12
  68.6 1.9 %collective-permute-done.5 = f32[13,32]{1,0:T(8,128)S(1)} collective-permute-done((f32[13,32]{1,0:T(8,128)S(1)}, f32[13,32]{1,0:T(8,128)S(1)}, u32[]{:S(2)}, u32[]{:S(2)}) %collective-permute-start.5) | collective-permute-done | bytes 1696 | tf_op jit(solution)/shard_map/ppermute | solution.py:12
  70.5 2.6 %collective-permute-start.6 = (f32[13,32]{1,0:T(8,128)S(1)}, f32[13,32]{1,0:T(8,128)S(1)}, u32[]{:S(2)}, u32[]{:S(2)}) collective-permute-start(f32[13,32]{1,0:T(8,128)S(1)} %add.171), channel_id=1, source_target_pairs={{0,4},{1,5},{2,6},{3,7},{4,0},{5,1},{6,2},{7,3},{8,12},{9,13},{10,... | collective-permute-start | bytes 5000 | tf_op jit(solution)/shard_map/ppermute | solution.py:12
  73.1 2.0 %collective-permute-done.6 = f32[13,32]{1,0:T(8,128)S(1)} collective-permute-done((f32[13,32]{1,0:T(8,128)S(1)}, f32[13,32]{1,0:T(8,128)S(1)}, u32[]{:S(2)}, u32[]{:S(2)}) %collective-permute-start.6) | collective-permute-done | bytes 1696 | tf_op jit(solution)/shard_map/ppermute | solution.py:12
  (98 shorter events, 31.6 us)
Async XLA Ops:
  0.6 9.5 %copy-start.1 = (f32[8,8,640]{2,1,0:T(8,128)S(1)}, f32[8,8,640]{2,1,0:T(8,128)}, u32[]{:S(2)}) copy-start(f32[8,8,640]{2,1,0:T(8,128)} %param.9) | copy-start | bytes 491524
  0.6 9.5 %copy-start = (f32[8,8,640]{2,1,0:T(8,128)S(1)}, f32[8,8,640]{2,1,0:T(8,128)}, u32[]{:S(2)}) copy-start(f32[8,8,640]{2,1,0:T(8,128)} %param.10) | copy-start | bytes 491524
  0.7 9.6 %copy-start.4 = (f32[8,8,640]{2,1,0:T(8,128)S(1)}, f32[8,8,640]{2,1,0:T(8,128)}, u32[]{:S(2)}) copy-start(f32[8,8,640]{2,1,0:T(8,128)} %param.11) | copy-start | bytes 491524
  1.6 5.2 %collective-permute-start.1 = (f32[2,2,8,640]{3,2,1,0:T(8,128)S(1)}, f32[2,2,8,640]{3,2,1,0:T(8,128)S(1)}, u32[]{:S(2)}, u32[]{:S(2)}) collective-permute-start(f32[2,2,8,640]{3,2,1,0:T(8,128)S(1)} %get-tuple-element.72), channel_id=1, source_target_pairs={{8,0},{16,8},{24,16},{0,24},{9,1},{17,9},{25,17},{1,25},{10,2},{18... | collective-permute-start | bytes 245768 | tf_op jit(solution)/shard_map/ppermute | solution.py:25
  4.0 3.9 %collective-permute-start = (f32[2,2,8,640]{3,2,1,0:T(8,128)S(1)}, f32[2,2,8,640]{3,2,1,0:T(8,128)S(1)}, u32[]{:S(2)}, u32[]{:S(2)}) collective-permute-start(f32[2,2,8,640]{3,2,1,0:T(8,128)S(1)} %get-tuple-element.73), channel_id=1, source_target_pairs={{0,8},{8,16},{16,24},{24,0},{1,9},{9,17},{17,25},{25,1},{2,10},{10... | collective-permute-start | bytes 245768 | tf_op jit(solution)/shard_map/ppermute | solution.py:24
  10.3 5.5 %collective-permute-start.2 = (f32[2,8,2,640]{3,2,1,0:T(2,128)S(1)}, f32[2,8,2,640]{3,2,1,0:T(2,128)S(1)}, u32[]{:S(2)}, u32[]{:S(2)}) collective-permute-start(f32[2,8,2,640]{3,2,1,0:T(2,128)S(1)} %get-tuple-element.68), channel_id=1, source_target_pairs={{0,1},{1,2},{2,3},{3,4},{4,5},{5,6},{6,7},{8,9},{9,10},{10,11},{11... | collective-permute-start | bytes 245768 | tf_op jit(solution)/shard_map/ppermute | solution.py:24
  13.8 6.3 %collective-permute-start.3 = (f32[2,8,2,640]{3,2,1,0:T(2,128)S(1)}, f32[2,8,2,640]{3,2,1,0:T(2,128)S(1)}, u32[]{:S(2)}, u32[]{:S(2)}) collective-permute-start(f32[2,8,2,640]{3,2,1,0:T(2,128)S(1)} %get-tuple-element.69), channel_id=1, source_target_pairs={{1,0},{2,1},{3,2},{4,3},{5,4},{6,5},{7,6},{9,8},{10,9},{11,10},{12... | collective-permute-start | bytes 245768 | tf_op jit(solution)/shard_map/ppermute | solution.py:25
  15.1 5.8 %copy-start.2 = (f32[8,8,640]{2,1,0:T(8,128)S(1)}, f32[8,8,640]{2,1,0:T(8,128)}, u32[]{:S(2)}) copy-start(f32[8,8,640]{2,1,0:T(8,128)} %param.12) | copy-start | bytes 491524
  20.3 1.0 %copy-start.3 = (s32[8,8,640]{2,1,0:T(8,128)S(1)}, s32[8,8,640]{2,1,0:T(8,128)}, u32[]{:S(2)}) copy-start(s32[8,8,640]{2,1,0:T(8,128)} %param.13) | copy-start | bytes 491524
  27.8 37.5 %copy-start.5 = (s32[1,32]{1,0:T(1,128)S(1)}, s32[1,32]{1,0:T(1,128)}, u32[]{:S(2)}) copy-start(s32[1,32]{1,0:T(1,128)} %param.15) | copy-start | bytes 388
  28.5 40.0 %copy-start.6 = (s32[1,32]{1,0:T(1,128)S(1)}, s32[1,32]{1,0:T(1,128)}, u32[]{:S(2)}) copy-start(s32[1,32]{1,0:T(1,128)} %param.14) | copy-start | bytes 388
  62.7 4.1 %collective-permute-start.4 = (f32[13,32]{1,0:T(8,128)S(1)}, f32[13,32]{1,0:T(8,128)S(1)}, u32[]{:S(2)}, u32[]{:S(2)}) collective-permute-start(f32[13,32]{1,0:T(8,128)S(1)} %get-tuple-element.30), channel_id=1, source_target_pairs={{0,1},{1,0},{2,3},{3,2},{4,5},{5,4},{6,7},{7,6},{8,9},{9,8},{10,11... | collective-permute-start | bytes 5000 | tf_op jit(solution)/shard_map/ppermute | solution.py:12
  66.9 3.7 %collective-permute-start.5 = (f32[13,32]{1,0:T(8,128)S(1)}, f32[13,32]{1,0:T(8,128)S(1)}, u32[]{:S(2)}, u32[]{:S(2)}) collective-permute-start(f32[13,32]{1,0:T(8,128)S(1)} %add.170), channel_id=1, source_target_pairs={{0,2},{1,3},{2,0},{3,1},{4,6},{5,7},{6,4},{7,5},{8,10},{9,11},{10,... | collective-permute-start | bytes 5000 | tf_op jit(solution)/shard_map/ppermute | solution.py:12
  70.5 4.5 %collective-permute-start.6 = (f32[13,32]{1,0:T(8,128)S(1)}, f32[13,32]{1,0:T(8,128)S(1)}, u32[]{:S(2)}, u32[]{:S(2)}) collective-permute-start(f32[13,32]{1,0:T(8,128)S(1)} %add.171), channel_id=1, source_target_pairs={{0,4},{1,5},{2,6},{3,7},{4,0},{5,1},{6,2},{7,3},{8,12},{9,13},{10,... | collective-permute-start | bytes 5000 | tf_op jit(solution)/shard_map/ppermute | solution.py:12
